TPU v7x, 32 devices: a whole 2x2x4 slice. The times are simulated.
32 devices in a mesh: section: 2 (over core), seq: 16 (over z, y, x).
Axes of the slice: x: 2, y: 2, z: 4, core: 2. Of those that a mesh axis runs over, the one named last changes fastest.
Arguments:
- queries: bfloat16 [4096, 4096], P('seq', 'section'), may hold values from -50 to 50
- key_rows: bfloat16 [4096, 4096], P('seq', 'section'), may hold values from -6 to 6
- value_rows: bfloat16 [4096, 4096], P('seq', 'section'), may hold values from -6 to 6
- block_pattern: int32 [32, 8], P('seq'), may hold values from 0 to 1, as said below
- out_weight: bfloat16 [4096, 4096], P('section'), may hold values from -0.09375 to 0.09375
- hidden: bfloat16 [4096, 4096], P('seq', 'section'), may hold values from -3 to 3
- norm_gain: float32 [4096], P('section'), may hold values from 0.5 to 1.5
Outputs:
- stream_out: bfloat16 [4096, 4096], P('seq', 'section')
- normed: bfloat16 [4096, 4096], P('seq', 'section')
Inputs may be any that keep to these rules, and one draw needn't show every extreme that they name: `block_pattern`: column 0 is 1 in every row: every query block attends its own block.
All inputs are finite; a program needn't handle non-finite values.
Results may differ from a plain program's by a relative error of at most 0.008.
Values may be sent and summed in bfloat16 or wider, within the bound.
A program may use at most 128 MiB of HBM per device.

v0:
```python
import functools
import math

import jax
import jax.numpy as jnp
from jax import lax
from jax.experimental import pallas as pl
from jax.experimental.pallas import tpu as pltpu
from jax.sharding import PartitionSpec as P

HEAD_DIM = 128
BLOCK = 128
WINDOW_BLOCKS = 8
GROUP = 4
FAR = 5
NEAR = -2
MESH = pl.DeviceIdType.MESH
HIDE = -1e30


def kernel(
    q_hbm, k_hbm, v_hbm, pattern, w_hbm, h_hbm,
    stream_ref, square_ref,
    kv, qbuf, wbuf, hbuf, bias, acc, mixed, mine, outgoing, incoming, square_out, square_in,
    own_sem, load_sem, send_sem, recv_sem, part_send, part_recv, sq_sem,
):
    rows, width = q_hbm.shape
    model = w_hbm.shape[1]
    subs = own_sem.shape[1]
    step_cols = width // subs
    piece = step_cols // 2
    shard = lax.axis_index("seq")
    section = lax.axis_index("section")
    count = lax.axis_size("seq")
    role = lax.rem(shard, GROUP)
    has_prev = shard >= GROUP
    has_next = shard + GROUP < count
    partner = 1 - section

    def base(off):
        return (FAR - off) * rows

    def view(off, k, part, tail):
        start = k * step_cols + (piece if part == 1 else 0)
        size = step_cols if part is None else piece
        cols = pl.ds(pl.multiple_of(start, piece), size)
        first, extent = (base(off) + rows - BLOCK, BLOCK) if tail else (base(off), rows)
        return kv.at[:, pl.ds(first, extent), cols]

    def part_index(part):
        return 1 if part == 1 else 0

    def send(index, k, off, target, to_off, part=None, tail=False):
        return pltpu.make_async_remote_copy(
            src_ref=view(off, k, part, tail),
            dst_ref=view(to_off, k, part, tail),
            send_sem=send_sem.at[index, k],
            recv_sem=recv_sem.at[to_off - NEAR, part_index(part), k],
            device_id={"seq": target},
            device_id_type=MESH,
        )

    def arrive(k, off, part=None, tail=False):
        pltpu.make_async_remote_copy(
            src_ref=view(off, k, part, tail),
            dst_ref=view(off, k, part, tail),
            send_sem=send_sem.at[0, k],
            recv_sem=recv_sem.at[off - NEAR, part_index(part), k],
            device_id={"section": partner},
            device_id_type=MESH,
        ).wait_recv()

    def own_loads(k):
        cols = pl.ds(pl.multiple_of(k * step_cols, step_cols), step_cols)
        return [
            pltpu.make_async_copy(
                source.at[:, cols], kv.at[i, pl.ds(base(0), rows), cols], own_sem.at[i, k]
            )
            for i, source in enumerate((k_hbm, v_hbm))
        ]

    table = [
        (
            [(0, 0, 2, 2, 0, False, None), (1, 0, 1, 1, 0, False, None),
             (2, 0, 2, 2, 1, False, None), (3, 0, 1, 1, 1, False, None),
             (4, 0, 4, 4, None, True, "next")],
            [([(-1, 0, False, None)],
              [(6, -1, 4, 3, 0, False, "next"), (5, -1, 2, 1, 0, False, None)]),
             ([(-2, 0, False, "next")], [(7, -2, 4, 2, 0, False, "next")])],
            [([(2, 0, False, "prev")], [(8, 2, 1, 3, 0, False, "prev")])],
            [(2, 1, False, "prev"), (3, 0, False, "prev"), (4, None, True, "prev"),
             (3, 1, False, "prev"), (1, 0, False, "prev"), (1, 1, False, "prev")],
        ),
        (
            [(0, 0, -1, -1, 0, False, None), (1, 0, 2, 2, 1, False, None),
             (2, 0, 4, 4, 1, False, "next"), (3, 0, 2, 2, 0, False, None),
             (4, 0, 4, 4, 0, True, "next")],
            [([(4, 1, False, "prev")], [(5, 4, -1, 3, 1, False, "prev")]),
             ([(-2, 1, False, "next")], [(8, -2, 4, 2, 1, False, "next")]),
             ([(1, 0, False, None)], [(6, 1, 2, 3, 0, False, None)])],
            [([(2, 0, False, "prev")], [(7, 2, -1, 1, 0, False, "prev")])],
            [(1, 1, False, None), (2, 1, False, "prev"), (4, 0, True, "prev"),
             (3, 0, False, "prev"), (3, 1, False, "prev")],
        ),
        (
            [(2, 0, 4, 4, 1, False, "next"), (0, 0, -2, -2, 0, False, "next"),
             (1, 0, 1, 1, 1, False, None), (3, 0, 1, 1, 0, False, None),
             (4, 0, 4, 4, 0, True, "next")],
            [([(4, 1, False, "prev")], [(5, 4, -2, 2, 1, False, "prev")]),
             ([(-1, 0, False, "next")], [(8, -1, 4, 3, 0, False, "next")]),
             ([(2, 1, False, None)], [(6, 2, 1, 3, 1, False, None)])],
            [([(3, 1, False, "prev")], [(7, 3, -2, 1, 1, False, "prev")])],
            [(2, 0, False, None), (3, 0, False, "prev"), (4, 0, True, "prev"),
             (1, 0, False, None), (1, 1, False, None)],
        ),
        (
            [(0, 0, 4, 4, 0, False, "next"), (2, 0, -2, -2, 1, False, "next"),
             (3, 0, -1, -1, 0, False, "next"), (1, 0, 4, 4, 1, False, "next")],
            [([(4, 0, False, "prev")], [(4, 4, -2, 2, 0, False, "prev")]),
             ([(4, 1, False, "prev")], [(5, 4, -1, 3, 1, False, "prev")]),
             ([(1, 1, False, None)], [(7, 1, 4, 5, 1, False, "next")]),
             ([(2, 1, False, None)], [(6, 2, -1, 1, 1, False, None)])],
            [([(5, 1, False, "prev")], [(8, 5, -2, 3, 1, False, "prev")])],
            [(2, 0, False, None), (1, 0, False, None),
             (3, 0, False, None), (3, 1, False, None)],
        ),
    ]

    def grouped(entries, act):
        for need in (None, "prev", "next"):
            chosen = [e for e in entries if e[-1] == need]
            if not chosen:
                continue
            if need is None:
                for e in chosen:
                    act(e)
            else:
                @pl.when(has_prev if need == "prev" else has_next)
                def _():
                    for e in chosen:
                        act(e)

    def start_sends(entries, k):
        def act(e):
            index, off, step, to_off, part, tail, _ = e
            send(index, k, off, shard + step, to_off, part, tail).start()

        grouped(entries, act)

    def end_sends(entries, k):
        def act(e):
            index, off, step, to_off, part, tail, _ = e
            send(index, k, off, shard + step, to_off, part, tail).wait_send()

        grouped(entries, act)

    def waits(entries, k):
        grouped(entries, lambda e: arrive(k, e[0], e[1], e[2]))

    def by_role(body):
        for r in range(GROUP):
            @pl.when(role == r)
            def _():
                body(table[r])

    def first_sends(k):
        for copy in own_loads(k):
            copy.wait()
        by_role(lambda row: start_sends(row[0], k))

    def relay(which, k):
        def body(row):
            for needed, sends in row[which]:
                waits(needed, k)
                start_sends(sends, k)

        by_role(body)

    q_load = pltpu.make_async_copy(q_hbm, qbuf, load_sem.at[0])
    w_load = pltpu.make_async_copy(w_hbm, wbuf, load_sem.at[1])
    h_load = pltpu.make_async_copy(h_hbm, hbuf, load_sem.at[2])

    for k in range(subs):
        for copy in own_loads(k):
            copy.start()
    q_load.start()
    w_load.start()
    h_load.start()

    barrier = pltpu.get_barrier_semaphore()
    across = jnp.where(lax.rem(role, 2) == 0, shard + 1, shard - 1)
    along = jnp.where(role < 2, shard + 2, shard - 2)
    pl.semaphore_signal(barrier, inc=1, device_id={"seq": across}, device_id_type=MESH)
    pl.semaphore_signal(barrier, inc=1, device_id={"seq": along}, device_id_type=MESH)
    pl.semaphore_signal(barrier, inc=1, device_id={"section": partner}, device_id_type=MESH)

    @pl.when(has_prev)
    def _():
        pl.semaphore_signal(
            barrier, inc=1, device_id={"seq": shard - GROUP}, device_id_type=MESH
        )

    @pl.when(has_next)
    def _():
        pl.semaphore_signal(
            barrier, inc=1, device_id={"seq": shard + GROUP}, device_id_type=MESH
        )

    pl.semaphore_wait(barrier, 3 + has_prev.astype(jnp.int32) + has_next.astype(jnp.int32))

    first_sends(0)

    for off in range(1, GROUP + 1):
        @pl.when(shard < off)
        def _():
            kv[:, pl.ds(base(off), rows), :] = jnp.zeros((2, rows, width), kv.dtype)

    query_place = lax.broadcasted_iota(jnp.int32, (BLOCK, BLOCK), 0)
    key_place = lax.broadcasted_iota(jnp.int32, (BLOCK, BLOCK), 1)
    blocks = rows // BLOCK
    span_blocks = WINDOW_BLOCKS - 1 + blocks
    for i in range(blocks):
        for g in range(span_blocks):
            j = i + WINDOW_BLOCKS - 1 - g
            if j < 0 or j >= WINDOW_BLOCKS:
                value = jnp.full((BLOCK, BLOCK), HIDE, jnp.float32)
            else:
                seen = (pattern[i, j] == 1) & (shard * blocks + i - j >= 0)
                level = jnp.where(seen, 0.0, HIDE).astype(jnp.float32)
                value = jnp.full((BLOCK, BLOCK), level, jnp.float32)
                if j == 0:
                    value = jnp.where(key_place <= query_place, value, HIDE)
            bias[i * BLOCK : (i + 1) * BLOCK, g * BLOCK : (g + 1) * BLOCK] = value
    acc[...] = jnp.zeros(acc.shape, acc.dtype)
    q_load.wait()
    w_load.wait()
    h_load.wait()

    key_first = base(GROUP) + rows - BLOCK
    key_span = span_blocks * BLOCK
    factor = math.log2(math.e) / math.sqrt(HEAD_DIM)
    tile = math.gcd(model, 1024)

    def heads(k):
        by_role(lambda row: waits(row[3], k))
        for n in range(step_cols // HEAD_DIM):
            cols = pl.ds(pl.multiple_of(k * step_cols + n * HEAD_DIM, HEAD_DIM), HEAD_DIM)
            query = qbuf[:, cols]
            keys = kv[0, pl.ds(key_first, key_span), cols]
            values = kv[1, pl.ds(key_first, key_span), cols]
            scores = lax.dot_general(
                query, keys, (((1,), (1,)), ((), ())), preferred_element_type=jnp.float32
            )
            scores = scores + bias[...]
            largest = jnp.max(scores, axis=1, keepdims=True)
            exponent = jnp.exp2((scores - largest) * factor)
            total = jnp.sum(exponent, axis=1, keepdims=True)
            mixture = jnp.dot(
                exponent.astype(jnp.bfloat16), values, preferred_element_type=jnp.float32
            )
            mixed[:, n * HEAD_DIM : (n + 1) * HEAD_DIM] = (mixture / total).astype(jnp.bfloat16)

    def attend(k):
        heads(k)
        depth = pl.ds(pl.multiple_of(k * step_cols, step_cols), step_cols)
        for c in range(0, model, tile):
            acc[:, c : c + tile] += jnp.dot(
                mixed[...], wbuf[depth, c : c + tile], preferred_element_type=jnp.float32
            )

    @pl.loop(0, subs)
    def _(t):
        @pl.when(t + 1 < subs)
        def _():
            first_sends(t + 1)

        relay(1, t)

        @pl.when(t >= 1)
        def _():
            relay(2, t - 1)

        @pl.when(t >= 3)
        def _():
            attend(t - 3)

    attend(subs - 3)
    relay(2, subs - 1)
    attend(subs - 2)
    heads(subs - 1)

    pieces = part_send.shape[0]
    part_cols = width // pieces

    def part_copy(c):
        cols = pl.ds(c * part_cols, part_cols)
        return pltpu.make_async_remote_copy(
            src_ref=outgoing.at[:, cols],
            dst_ref=incoming.at[:, cols],
            send_sem=part_send.at[c],
            recv_sem=part_recv.at[c],
            device_id={"section": partner},
            device_id_type=MESH,
        )

    last = pl.ds((subs - 1) * step_cols, step_cols)

    def last_sum(start):
        cols = pl.ds(pl.multiple_of(start, part_cols), part_cols)
        return acc[:, cols] + jnp.dot(
            mixed[...], wbuf[last, cols], preferred_element_type=jnp.float32
        )

    for c in range(pieces):
        outgoing[:, c * part_cols : (c + 1) * part_cols] = last_sum(
            partner * width + c * part_cols
        ).astype(outgoing.dtype)
        if c >= 1:
            part_copy(c - 1).start()
    for c in range(pieces):
        cols = slice(c * part_cols, (c + 1) * part_cols)
        mine[:, cols] = last_sum(section * width + c * part_cols).astype(mine.dtype)
        if c == 0:
            part_copy(pieces - 1).start()
    for c in range(pieces):
        part_copy(c).wait_recv()

    strip = 16

    @pl.loop(0, rows // strip)
    def _(i):
        place = pl.ds(pl.multiple_of(i * strip, strip), strip)
        here = mine[place, :].astype(jnp.float32)
        there = incoming[place, :].astype(jnp.float32)
        stream = hbuf[place, :].astype(jnp.float32) + (here + there)
        stream_ref[place, :] = stream
        squares = stream * stream
        lanes = squares[:, 0:128]
        for c in range(128, width, 128):
            lanes = lanes + squares[:, c : c + 128]
        square_out[place, :] = lanes

    square_copy = pltpu.make_async_remote_copy(
        src_ref=square_out,
        dst_ref=square_in,
        send_sem=sq_sem.at[0],
        recv_sem=sq_sem.at[1],
        device_id={"section": partner},
        device_id_type=MESH,
    )
    square_copy.start()

    @pl.loop(0, subs)
    def _(k):
        def body(row):
            end_sends(row[0], k)
            for which in (1, 2):
                for _, sends in row[which]:
                    end_sends(sends, k)

        by_role(body)

    for c in range(pieces):
        part_copy(c).wait_send()
    square_copy.wait()
    square_ref[...] = square_out[...] + square_in[...]


def shards(queries, key_rows, value_rows, block_pattern, out_weight, hidden, norm_gain):
    rows, width = queries.shape
    model = out_weight.shape[1]
    subs = width // (2 * HEAD_DIM)
    pieces = 4
    span = (WINDOW_BLOCKS - 1) * BLOCK + rows
    anywhere = pl.BlockSpec(memory_space=pl.ANY)
    vmem = pl.BlockSpec(memory_space=pltpu.VMEM)
    stream, squares = pl.pallas_call(
        kernel,
        out_shape=(
            jax.ShapeDtypeStruct((rows, width), jnp.float32),
            jax.ShapeDtypeStruct((rows, 128), jnp.float32),
        ),
        in_specs=[
            anywhere, anywhere, anywhere,
            pl.BlockSpec(memory_space=pltpu.SMEM),
            anywhere, anywhere,
        ],
        out_specs=(vmem, vmem),
        scratch_shapes=[
            pltpu.VMEM((2, (FAR + 1 - NEAR) * rows, width), jnp.bfloat16),
            pltpu.VMEM((rows, width), jnp.bfloat16),
            pltpu.VMEM((width, model), jnp.bfloat16),
            pltpu.VMEM((rows, width), jnp.bfloat16),
            pltpu.VMEM((rows, span), jnp.float32),
            pltpu.VMEM((rows, model), jnp.float32),
            pltpu.VMEM((rows, 2 * HEAD_DIM), jnp.bfloat16),
            pltpu.VMEM((rows, width), jnp.bfloat16),
            pltpu.VMEM((rows, width), jnp.bfloat16),
            pltpu.VMEM((rows, width), jnp.bfloat16),
            pltpu.VMEM((rows, 128), jnp.float32),
            pltpu.VMEM((rows, 128), jnp.float32),
            pltpu.SemaphoreType.DMA((2, subs)),
            pltpu.SemaphoreType.DMA((3,)),
            pltpu.SemaphoreType.DMA((9, subs)),
            pltpu.SemaphoreType.DMA((FAR + 1 - NEAR, 2, subs)),
            pltpu.SemaphoreType.DMA((pieces,)),
            pltpu.SemaphoreType.DMA((pieces,)),
            pltpu.SemaphoreType.DMA((2,)),
        ],
        compiler_params=pltpu.CompilerParams(
            collective_id=0, has_side_effects=True, vmem_limit_bytes=62 * 1024 * 1024
        ),
    )(queries, key_rows, value_rows, block_pattern, out_weight, hidden)
    mean_square = jnp.sum(squares, axis=1, keepdims=True) / model
    normed = stream * lax.rsqrt(mean_square + 1e-06) * norm_gain[None, :]
    return (stream.astype(jnp.bfloat16), normed.astype(jnp.bfloat16))


def solution(mesh):
    placed = (
        P("seq", "section"),
        P("seq", "section"),
        P("seq", "section"),
        P("seq", None),
        P("section", None),
        P("seq", "section"),
        P("section"),
    )
    return jax.shard_map(
        shards,
        mesh=mesh,
        in_specs=placed,
        out_specs=(P("seq", "section"), P("seq", "section")),
        check_vma=False,
    )
```

profile of v0, /device:TPU:27, one launch (start us, length us, event | category | flops | bytes accessed | tf_op | source)
XLA Modules:
  0.0 92.6 jit_solution(18011184428929083007)
XLA Ops:
  0.6 0.0 copy-start
  0.6 87.1 %shard_map.86 = (f32[256,2048]{1,0:T(8,128)}, f32[256,128]{1,0:T(8,128)}) custom-call(bf16[256,2048]{1,0:T(8,128)(2,1)} %q_hbm.1, bf16[256,2048]{1,0:T(8,128)(2,1)} %k_hbm.1, bf16[256,2048]{1,0:T(8,128)(2,1)} %v_hbm.1, s32[2,8]{1,0:T(2,128)} %pattern.1, bf16[2048,4096]{1,0:T(8,128)(2,1)} %w_hbm.1, bf16[256,2048]{1,0:T(8,128)(2,1)} %h_hbm.1), custom_call_target="tpu_custom_call" | custom-call | tf_op jit(solution)/shard_map/pallas_call | solution.py:377
  87.7 1.0 %reduce_sum.9 = f32[256]{0:T(256)S(1)} reduce(f32[256,128]{1,0:T(8,128)} %get-tuple-element.5, f32[]{:T(128)} %constant.1.clone.1), dimensions={1}, to_apply=%region_0.0 | reduce | flops 32512 | bytes 132100 | tf_op jit(solution)/shard_map/reduce_sum | solution.py:414
  88.8 0.0 copy-done
  88.8 3.8 %multiply_convert_fusion = (bf16[256,2048]{1,0:T(8,128)(2,1)}, bf16[256,2048]{1,0:T(8,128)(2,1)}) fusion(f32[256,2048]{1,0:T(8,128)} %get-tuple-element.4, f32[2048]{0:T(1024)S(1)} %copy-done, f32[256]{0:T(256)S(1)} %add_rsqrt_fusion), kind=kLoop, calls=%fused_computation | loop fusion | flops 2097152 | bytes 4203520 | tf_op jit(solution)/shard_map/convert_element_type | solution.py:416
  (1 shorter events, 0.0 us)
Async XLA Ops:
  0.6 88.1 %copy-start = (f32[2048]{0:T(1024)S(1)}, f32[2048]{0:T(1024)}, u32[]{:S(2)}) copy-start(f32[2048]{0:T(1024)} %param.13) | copy-start | bytes 24580
where the time goes:
time: 92.7 us; the launch traced here: 92.6 us
  Pallas kernels  87.1 us (94%)
  other arithmetic  4.8 us (5%)
    pallas_call x1, Pallas kernels, shards(): pl.pallas_call(kernel, out_shape=(jax.ShapeDtypeStruct((rows, width), jnp...  87.1 us
    convert_element_type x1, other arithmetic, shards(): return (stream.astype(jnp.bfloat16), normed.astype(jnp.bfloat16))  3.78 us

commit v1 on v0

v1 whole, which is shorter than its diff:
```python
import math

import jax
import jax.numpy as jnp
from jax import lax
from jax.experimental import pallas as pl
from jax.experimental.pallas import tpu as pltpu
from jax.sharding import PartitionSpec as P

HEAD_DIM = 128
BLOCK = 128
WINDOW_BLOCKS = 8
GROUP = 4
MESH = pl.DeviceIdType.MESH
HIDE = -1e30


def kernel(
    q_hbm, k_hbm, v_hbm, pattern_hbm, w_hbm, h_hbm,
    stream_ref, square_ref,
    kv, qbuf, obuf, amix, wbuf, hbuf, patterns, bias, acc,
    mine, outgoing, incoming, square_out, square_in,
    kv_own, q_own, pat_own, w_sem, h_sem,
    kv_send, kv_recv, z_send, q_send, q_recv, o_send, o_recv, pat_send, pat_recv,
    part_send, part_recv, sq_sem,
):
    rows, width = q_hbm.shape
    model = w_hbm.shape[1]
    heads = kv.shape[1]
    blocks = rows // BLOCK
    front = (WINDOW_BLOCKS - 1) * BLOCK
    span = front + rows
    skip = GROUP * rows - front
    shard = lax.axis_index("seq")
    section = lax.axis_index("section")
    count = lax.axis_size("seq")
    role = lax.rem(shard, GROUP)
    first_shard = shard - role
    has_prev = shard >= GROUP
    has_next = shard + GROUP < count
    partner = 1 - section
    low = lax.rem(role, 2)
    high = role // 2
    peers = (3 - role, 2 * high + 1 - low, 2 * (1 - high) + low)
    sources = (k_hbm, v_hbm)

    def head_cols(home, n):
        return pl.ds(pl.multiple_of((home * heads + n) * HEAD_DIM, HEAD_DIM), HEAD_DIM)

    def place(slot):
        return pl.ds(pl.multiple_of(slot * rows, rows), rows)

    def to_peer(peer):
        return {"seq": first_shard + peer}

    def kv_local(i, n):
        return pltpu.make_async_copy(
            sources[i].at[:, head_cols(role, n)],
            kv.at[i, n, place(GROUP + role), :],
            kv_own.at[i, n],
        )

    def q_local(n):
        return pltpu.make_async_copy(
            q_hbm.at[:, head_cols(role, n)], qbuf.at[n, place(role), :], q_own.at[n]
        )

    def kv_copy(i, n, e):
        return pltpu.make_async_remote_copy(
            src_ref=sources[i].at[:, head_cols(peers[e], n)],
            dst_ref=kv.at[i, n, place(GROUP + role), :],
            send_sem=kv_send.at[i, n, e],
            recv_sem=kv_recv.at[i, n, GROUP + role],
            device_id=to_peer(peers[e]),
            device_id_type=MESH,
        )

    def kv_arrive(i, n, slot):
        pltpu.make_async_remote_copy(
            src_ref=kv.at[i, n, place(slot), :],
            dst_ref=kv.at[i, n, place(slot), :],
            send_sem=kv_send.at[i, n, 0],
            recv_sem=kv_recv.at[i, n, slot],
            device_id={"section": partner},
            device_id_type=MESH,
        ).wait_recv()

    def q_copy(n, e):
        return pltpu.make_async_remote_copy(
            src_ref=q_hbm.at[:, head_cols(peers[e], n)],
            dst_ref=qbuf.at[n, place(role), :],
            send_sem=q_send.at[n, e],
            recv_sem=q_recv.at[n, role],
            device_id=to_peer(peers[e]),
            device_id_type=MESH,
        )

    def q_arrive(n, c):
        pltpu.make_async_remote_copy(
            src_ref=qbuf.at[n, place(c), :],
            dst_ref=qbuf.at[n, place(c), :],
            send_sem=q_send.at[n, 0],
            recv_sem=q_recv.at[n, c],
            device_id={"section": partner},
            device_id_type=MESH,
        ).wait_recv()

    def mix_cols(c):
        return pl.ds(pl.multiple_of(c * HEAD_DIM, HEAD_DIM), HEAD_DIM)

    def o_copy(n, c):
        return pltpu.make_async_remote_copy(
            src_ref=obuf.at[n, place(c), :],
            dst_ref=amix.at[n, :, mix_cols(role)],
            send_sem=o_send.at[n, c],
            recv_sem=o_recv.at[n, role],
            device_id=to_peer(c),
            device_id_type=MESH,
        )

    def o_arrive(n, c):
        pltpu.make_async_remote_copy(
            src_ref=amix.at[n, :, mix_cols(c)],
            dst_ref=amix.at[n, :, mix_cols(c)],
            send_sem=o_send.at[n, 0],
            recv_sem=o_recv.at[n, c],
            device_id={"section": partner},
            device_id_type=MESH,
        ).wait_recv()

    def pat_copy(e):
        return pltpu.make_async_remote_copy(
            src_ref=pattern_hbm,
            dst_ref=patterns.at[role],
            send_sem=pat_send.at[e],
            recv_sem=pat_recv.at[role],
            device_id=to_peer(peers[e]),
            device_id_type=MESH,
        )

    def pat_arrive(c):
        pltpu.make_async_remote_copy(
            src_ref=patterns.at[c],
            dst_ref=patterns.at[c],
            send_sem=pat_send.at[0],
            recv_sem=pat_recv.at[c],
            device_id={"section": partner},
            device_id_type=MESH,
        ).wait_recv()

    def z_copies(i, n, c, own):
        def one(first, extent):
            if own:
                source = sources[i].at[pl.ds(first, extent), head_cols(role, n)]
            else:
                source = kv.at[
                    i, n, pl.ds(pl.multiple_of((GROUP + c) * rows + first, BLOCK), extent), :
                ]
            return pltpu.make_async_remote_copy(
                src_ref=source,
                dst_ref=kv.at[i, n, pl.ds(pl.multiple_of(c * rows + first, BLOCK), extent), :],
                send_sem=z_send.at[i, n, c],
                recv_sem=kv_recv.at[i, n, c],
                device_id={"seq": shard + GROUP},
                device_id_type=MESH,
            )

        return one(skip, rows - skip), one(0, rows)

    def z_act(i, n, c, own, act):
        tail, full = z_copies(i, n, c, own)

        @pl.when(has_next & (c == 0))
        def _():
            act(tail)

        @pl.when(has_next & (c > 0))
        def _():
            act(full)

    def z_start(i, n, c, own):
        z_act(i, n, c, own, lambda copy: copy.start())

    def z_end(i, n, c):
        z_act(i, n, c, False, lambda copy: copy.wait_send())

    def z_arrive(n, c):
        @pl.when(has_prev)
        def _():
            for i in range(2):
                tail = pl.ds(c * rows + (skip if c == 0 else 0), rows - (skip if c == 0 else 0))
                pltpu.make_async_remote_copy(
                    src_ref=kv.at[i, n, tail, :],
                    dst_ref=kv.at[i, n, tail, :],
                    send_sem=z_send.at[i, n, 0],
                    recv_sem=kv_recv.at[i, n, c],
                    device_id={"section": partner},
                    device_id_type=MESH,
                ).wait_recv()

    def w_copy(n, c):
        return pltpu.make_async_copy(
            w_hbm.at[pl.ds((c * heads + n) * HEAD_DIM, HEAD_DIM), :],
            wbuf.at[pl.ds((n * GROUP + c) * HEAD_DIM, HEAD_DIM), :],
            w_sem.at[n, c],
        )

    h_load = pltpu.make_async_copy(h_hbm, hbuf, h_sem.at[0])
    pat_load = pltpu.make_async_copy(pattern_hbm, patterns.at[role], pat_own.at[0])

    barrier = pltpu.get_barrier_semaphore()
    for e in range(GROUP - 1):
        pl.semaphore_signal(barrier, inc=1, device_id=to_peer(peers[e]), device_id_type=MESH)
    pl.semaphore_signal(barrier, inc=1, device_id={"section": partner}, device_id_type=MESH)

    @pl.when(has_prev)
    def _():
        pl.semaphore_signal(
            barrier, inc=1, device_id={"seq": shard - GROUP}, device_id_type=MESH
        )

    @pl.when(has_next)
    def _():
        pl.semaphore_signal(
            barrier, inc=1, device_id={"seq": shard + GROUP}, device_id_type=MESH
        )

    pat_load.start()
    for n in range(heads):
        for i in range(2):
            kv_local(i, n).start()
        q_local(n).start()

    pl.semaphore_wait(
        barrier, GROUP + has_prev.astype(jnp.int32) + has_next.astype(jnp.int32)
    )

    for e in range(GROUP - 1):
        pat_copy(e).start()
    for n in range(heads):
        for i in range(2):
            for e in range(GROUP - 1):
                kv_copy(i, n, e).start()
            if n < 2:
                z_start(i, n, role, True)
        for e in range(GROUP - 1):
            q_copy(n, e).start()
    for n in range(heads):
        for c in range(GROUP):
            w_copy(n, c).start()
    h_load.start()

    @pl.when(jnp.logical_not(has_prev))
    def _():
        for n in range(heads):
            kv[:, n, 0 : GROUP * rows, :] = jnp.zeros((2, GROUP * rows, HEAD_DIM), kv.dtype)

    pat_load.wait()
    for e in range(GROUP - 1):
        pat_arrive(peers[e])

    query_place = lax.broadcasted_iota(jnp.int32, (BLOCK, BLOCK), 0)
    key_place = lax.broadcasted_iota(jnp.int32, (BLOCK, BLOCK), 1)
    span_blocks = span // BLOCK
    for c in range(GROUP):
        for i in range(blocks):
            for g in range(span_blocks):
                j = i + WINDOW_BLOCKS - 1 - g
                if j < 0 or j >= WINDOW_BLOCKS:
                    value = jnp.full((BLOCK, BLOCK), HIDE, jnp.float32)
                else:
                    valid = (first_shard + c) * blocks + i - j >= 0
                    floor = jnp.where(valid, 0.0, HIDE).astype(jnp.float32)
                    level = jnp.where(patterns[c, i : i + 1, j : j + 1] == 1, floor, HIDE)
                    value = jnp.broadcast_to(level, (BLOCK, BLOCK))
                    if j == 0:
                        value = jnp.where(key_place <= query_place, value, HIDE)
                bias[c, i * BLOCK : (i + 1) * BLOCK, g * BLOCK : (g + 1) * BLOCK] = value

    factor = math.log2(math.e) / math.sqrt(HEAD_DIM)
    tile = math.gcd(model, 1024)

    def forward(n):
        for i in range(2):
            kv_local(i, n).wait()
        for e in (1, 2, 0):
            for i in range(2):
                kv_arrive(i, n, GROUP + peers[e])
                z_start(i, n, peers[e], False)

        @pl.when(n + 2 < heads)
        def _():
            for i in range(2):
                z_start(i, jnp.minimum(n + 2, heads - 1), role, True)

    def unit(n, c):
        @pl.when(c == role)
        def _():
            q_local(n).wait()

        @pl.when(c != role)
        def _():
            q_arrive(n, c)

        z_arrive(n, c)
        keys_at = pl.ds(c * rows + skip, span)
        query = qbuf[n, c * rows : (c + 1) * rows, :]
        scores = lax.dot_general(
            query, kv[0, n, keys_at, :], (((1,), (1,)), ((), ())),
            preferred_element_type=jnp.float32,
        )
        scores = scores + bias[c]
        largest = jnp.max(scores, axis=1, keepdims=True)
        exponent = jnp.exp2((scores - largest) * factor)
        total = jnp.sum(exponent, axis=1, keepdims=True)
        mixture = jnp.dot(
            exponent.astype(jnp.bfloat16), kv[1, n, keys_at, :],
            preferred_element_type=jnp.float32,
        )
        result = (mixture / total).astype(jnp.bfloat16)

        @pl.when(c == role)
        def _():
            amix[n, :, mix_cols(c)] = result

        @pl.when(c != role)
        def _():
            obuf[n, c * rows : (c + 1) * rows, :] = result
            o_copy(n, c).start()

    def mixed_ready(n):
        for e in range(GROUP - 1):
            o_arrive(n, peers[e])

    def depth(n):
        return pl.ds(pl.multiple_of(n * GROUP * HEAD_DIM, GROUP * HEAD_DIM), GROUP * HEAD_DIM)

    def project(n, first):
        for c in range(GROUP):
            w_copy(n, c).wait()
        mixed_ready(n)
        for t in range(0, model, tile):
            value = jnp.dot(
                amix[n], wbuf[depth(n), t : t + tile], preferred_element_type=jnp.float32
            )
            if first:
                acc[:, t : t + tile] = value
            else:
                acc[:, t : t + tile] += value

    @pl.loop(0, heads)
    def _(t):
        forward(t)

        @pl.when(t >= 1)
        def _():
            for c in reversed(range(GROUP)):
                unit(t - 1, c)

    last_head = heads - 1
    for c in reversed(range(GROUP)):
        unit(last_head, c)
    for n in range(last_head):
        project(n, n == 0)
    h_load.wait()
    for c in range(GROUP):
        w_copy(last_head, c).wait()
    mixed_ready(last_head)

    pieces = part_send.shape[0]
    part_cols = width // pieces

    def part_copy(c):
        cols = pl.ds(c * part_cols, part_cols)
        return pltpu.make_async_remote_copy(
            src_ref=outgoing.at[:, cols],
            dst_ref=incoming.at[:, cols],
            send_sem=part_send.at[c],
            recv_sem=part_recv.at[c],
            device_id={"section": partner},
            device_id_type=MESH,
        )

    def last_sum(start):
        cols = pl.ds(pl.multiple_of(start, part_cols), part_cols)
        return acc[:, cols] + jnp.dot(
            amix[last_head], wbuf[depth(last_head), cols], preferred_element_type=jnp.float32
        )

    for c in range(pieces):
        outgoing[:, c * part_cols : (c + 1) * part_cols] = last_sum(
            partner * width + c * part_cols
        ).astype(outgoing.dtype)
        if c >= 1:
            part_copy(c - 1).start()
    for c in range(pieces):
        cols = slice(c * part_cols, (c + 1) * part_cols)
        mine[:, cols] = last_sum(section * width + c * part_cols).astype(mine.dtype)
        if c == 0:
            part_copy(pieces - 1).start()
    for c in range(pieces):
        part_copy(c).wait_recv()

    strip = 16

    @pl.loop(0, rows // strip)
    def _(i):
        at = pl.ds(pl.multiple_of(i * strip, strip), strip)
        here = mine[at, :].astype(jnp.float32)
        there = incoming[at, :].astype(jnp.float32)
        stream = hbuf[at, :].astype(jnp.float32) + (here + there)
        stream_ref[at, :] = stream
        squares = stream * stream
        lanes = squares[:, 0:128]
        for c in range(128, width, 128):
            lanes = lanes + squares[:, c : c + 128]
        square_out[at, :] = lanes

    square_copy = pltpu.make_async_remote_copy(
        src_ref=square_out,
        dst_ref=square_in,
        send_sem=sq_sem.at[0],
        recv_sem=sq_sem.at[1],
        device_id={"section": partner},
        device_id_type=MESH,
    )
    square_copy.start()

    for e in range(GROUP - 1):
        pat_copy(e).wait_send()

    @pl.loop(0, heads)
    def _(n):
        for e in range(GROUP - 1):
            for i in range(2):
                kv_copy(i, n, e).wait_send()
            q_copy(n, e).wait_send()
            o_copy(n, peers[e]).wait_send()
        for i in range(2):
            for c in range(GROUP):
                z_end(i, n, c)

    for c in range(pieces):
        part_copy(c).wait_send()
    square_copy.wait()
    square_ref[...] = square_out[...] + square_in[...]


def shards(queries, key_rows, value_rows, block_pattern, out_weight, hidden, norm_gain):
    rows, width = queries.shape
    model = out_weight.shape[1]
    heads = width // (GROUP * HEAD_DIM)
    pieces = 4
    span = (WINDOW_BLOCKS - 1) * BLOCK + rows
    anywhere = pl.BlockSpec(memory_space=pl.ANY)
    vmem = pl.BlockSpec(memory_space=pltpu.VMEM)
    bf16 = jnp.bfloat16
    stream, squares = pl.pallas_call(
        kernel,
        out_shape=(
            jax.ShapeDtypeStruct((rows, width), jnp.float32),
            jax.ShapeDtypeStruct((rows, 128), jnp.float32),
        ),
        in_specs=[anywhere] * 6,
        out_specs=(vmem, vmem),
        scratch_shapes=[
            pltpu.VMEM((2, heads, 2 * GROUP * rows, HEAD_DIM), bf16),
            pltpu.VMEM((heads, GROUP * rows, HEAD_DIM), bf16),
            pltpu.VMEM((heads, GROUP * rows, HEAD_DIM), bf16),
            pltpu.VMEM((heads, rows, GROUP * HEAD_DIM), bf16),
            pltpu.VMEM((width, model), bf16),
            pltpu.VMEM((rows, width), bf16),
            pltpu.VMEM((GROUP,) + block_pattern.shape, jnp.int32),
            pltpu.VMEM((GROUP, rows, span), jnp.float32),
            pltpu.VMEM((rows, model), jnp.float32),
            pltpu.VMEM((rows, width), bf16),
            pltpu.VMEM((rows, width), bf16),
            pltpu.VMEM((rows, width), bf16),
            pltpu.VMEM((rows, 128), jnp.float32),
            pltpu.VMEM((rows, 128), jnp.float32),
            pltpu.SemaphoreType.DMA((2, heads)),
            pltpu.SemaphoreType.DMA((heads,)),
            pltpu.SemaphoreType.DMA((1,)),
            pltpu.SemaphoreType.DMA((heads, GROUP)),
            pltpu.SemaphoreType.DMA((1,)),
            pltpu.SemaphoreType.DMA((2, heads, GROUP - 1)),
            pltpu.SemaphoreType.DMA((2, heads, 2 * GROUP)),
            pltpu.SemaphoreType.DMA((2, heads, GROUP)),
            pltpu.SemaphoreType.DMA((heads, GROUP - 1)),
            pltpu.SemaphoreType.DMA((heads, GROUP)),
            pltpu.SemaphoreType.DMA((heads, GROUP)),
            pltpu.SemaphoreType.DMA((heads, GROUP)),
            pltpu.SemaphoreType.DMA((GROUP - 1,)),
            pltpu.SemaphoreType.DMA((GROUP,)),
            pltpu.SemaphoreType.DMA((pieces,)),
            pltpu.SemaphoreType.DMA((pieces,)),
            pltpu.SemaphoreType.DMA((2,)),
        ],
        compiler_params=pltpu.CompilerParams(
            collective_id=0, has_side_effects=True, vmem_limit_bytes=62 * 1024 * 1024
        ),
    )(queries, key_rows, value_rows, block_pattern, out_weight, hidden)
    mean_square = jnp.sum(squares, axis=1, keepdims=True) / model
    normed = stream * lax.rsqrt(mean_square + 1e-06) * norm_gain[None, :]
    return (stream.astype(jnp.bfloat16), normed.astype(jnp.bfloat16))


def solution(mesh):
    placed = (
        P("seq", "section"),
        P("seq", "section"),
        P("seq", "section"),
        P("seq", None),
        P("section", None),
        P("seq", "section"),
        P("section"),
    )
    return jax.shard_map(
        shards,
        mesh=mesh,
        in_specs=placed,
        out_specs=(P("seq", "section"), P("seq", "section")),
        check_vma=False,
    )
```

time: 92.7 us -> 66.9 us (0.72)
  the two profiles are of different devices: /device:TPU:27 before, /device:TPU:25 now
where the time goes in v1:
time: 66.9 us; the launch traced here: 66.7 us
  Pallas kernels  61.2 us (91%)
  other arithmetic  4.8 us (7%)
  between operations  0.67 us (1%)
    pallas_call x1, Pallas kernels, shards(): pl.pallas_call(kernel, out_shape=(jax.ShapeDtypeStruct((rows, width), jnp...  61.2 us
    convert_element_type x1, other arithmetic, shards(): return (stream.astype(jnp.bfloat16), normed.astype(jnp.bfloat16))  3.78 us

profile of v1, /device:TPU:25, one launch (start us, length us, event | category | flops | bytes accessed | tf_op | source)
XLA Modules:
  0.0 66.7 jit_solution(13419216320941229076)
XLA Ops:
  0.6 0.0 copy-start
  0.6 61.2 %shard_map.86 = (f32[256,2048]{1,0:T(8,128)}, f32[256,128]{1,0:T(8,128)}) custom-call(bf16[256,2048]{1,0:T(8,128)(2,1)} %q_hbm.1, bf16[256,2048]{1,0:T(8,128)(2,1)} %k_hbm.1, bf16[256,2048]{1,0:T(8,128)(2,1)} %v_hbm.1, s32[2,8]{1,0:T(2,128)} %pattern_hbm.1, bf16[2048,4096]{1,0:T(8,128)(2,1)} %w_hbm.1, bf16[256,2048]{1,0:T(8,128)(2,1)} %h_hbm.1), custom_call_target="tpu_custom_call" | custom-call | tf_op jit(solution)/shard_map/pallas_call | solution.py:458
  61.9 1.0 %reduce_sum.9 = f32[256]{0:T(256)S(1)} reduce(f32[256,128]{1,0:T(8,128)} %get-tuple-element.5, f32[]{:T(128)} %constant.1.clone.1), dimensions={1}, to_apply=%region_0.0 | reduce | flops 32512 | bytes 132100 | tf_op jit(solution)/shard_map/reduce_sum | solution.py:503
  62.9 0.0 copy-done
  62.9 3.8 %multiply_convert_fusion = (bf16[256,2048]{1,0:T(8,128)(2,1)}, bf16[256,2048]{1,0:T(8,128)(2,1)}) fusion(f32[256,2048]{1,0:T(8,128)} %get-tuple-element.4, f32[2048]{0:T(1024)S(1)} %copy-done, f32[256]{0:T(256)S(1)} %add_rsqrt_fusion), kind=kLoop, calls=%fused_computation | loop fusion | flops 2097152 | bytes 4203520 | tf_op jit(solution)/shard_map/convert_element_type | solution.py:505
  (1 shorter events, 0.0 us)
Async XLA Ops:
  0.6 62.3 %copy-start = (f32[2048]{0:T(1024)S(1)}, f32[2048]{0:T(1024)}, u32[]{:S(2)}) copy-start(f32[2048]{0:T(1024)} %param.13) | copy-start | bytes 24580

commit v2 on v1

--- a/solution.py
+++ b/solution.py
@@ -18,14 +18,13 @@
 def kernel(
     q_hbm, k_hbm, v_hbm, pattern_hbm, w_hbm, h_hbm,
     stream_ref, square_ref,
-    kv, qbuf, obuf, amix, wbuf, hbuf, patterns, bias, acc,
-    mine, outgoing, incoming, square_out, square_in,
-    kv_own, q_own, pat_own, w_sem, h_sem,
+    kv, qbuf, obuf, amix, wbuf, hbuf, patterns, bias, acc, square_out, square_in,
+    kv_own, q_own, pat_own, w_own, w_send, w_recv, h_sem,
     kv_send, kv_recv, z_send, q_send, q_recv, o_send, o_recv, pat_send, pat_recv,
-    part_send, part_recv, sq_sem,
+    mix_send, mix_recv, sq_sem, entered,
 ):
     rows, width = q_hbm.shape
-    model = w_hbm.shape[1]
+    features = h_hbm.shape[1]
     heads = kv.shape[1]
     blocks = rows // BLOCK
     front = (WINDOW_BLOCKS - 1) * BLOCK
@@ -111,7 +110,7 @@
     def o_copy(n, c):
         return pltpu.make_async_remote_copy(
             src_ref=obuf.at[n, place(c), :],
-            dst_ref=amix.at[n, :, mix_cols(role)],
+            dst_ref=amix.at[0, n, :, mix_cols(role)],
             send_sem=o_send.at[n, c],
             recv_sem=o_recv.at[n, role],
             device_id=to_peer(c),
@@ -120,8 +119,8 @@
 
     def o_arrive(n, c):
         pltpu.make_async_remote_copy(
-            src_ref=amix.at[n, :, mix_cols(c)],
-            dst_ref=amix.at[n, :, mix_cols(c)],
+            src_ref=amix.at[0, n, :, mix_cols(c)],
+            dst_ref=amix.at[0, n, :, mix_cols(c)],
             send_sem=o_send.at[n, 0],
             recv_sem=o_recv.at[n, c],
             device_id={"section": partner},
@@ -198,18 +197,45 @@
                     device_id_type=MESH,
                 ).wait_recv()
 
+    def w_part(n, c, owner):
+        return w_hbm.at[
+            pl.ds((c * heads + n) * HEAD_DIM, HEAD_DIM),
+            pl.ds(pl.multiple_of(owner * features, features), features),
+        ]
+
+    def w_local(n, c):
+        return pltpu.make_async_copy(
+            w_part(n, c, section),
+            wbuf.at[0, n, c * HEAD_DIM : (c + 1) * HEAD_DIM, :],
+            w_own.at[n, c],
+        )
+
     def w_copy(n, c):
-        return pltpu.make_async_copy(
-            w_hbm.at[pl.ds((c * heads + n) * HEAD_DIM, HEAD_DIM), :],
-            wbuf.at[pl.ds((n * GROUP + c) * HEAD_DIM, HEAD_DIM), :],
-            w_sem.at[n, c],
+        return pltpu.make_async_remote_copy(
+            src_ref=w_part(n, c, partner),
+            dst_ref=wbuf.at[1, n, c * HEAD_DIM : (c + 1) * HEAD_DIM, :],
+            send_sem=w_send.at[n, c],
+            recv_sem=w_recv.at[n, c],
+            device_id={"section": partner},
+            device_id_type=MESH,
+        )
+
+    def mix_copy(n, first, extent):
+        cols = pl.ds(first * HEAD_DIM, extent * HEAD_DIM)
+        return pltpu.make_async_remote_copy(
+            src_ref=amix.at[0, n, :, cols],
+            dst_ref=amix.at[1, n, :, cols],
+            send_sem=mix_send.at[n, first],
+            recv_sem=mix_recv.at[n, first],
+            device_id={"section": partner},
+            device_id_type=MESH,
         )
 
     h_load = pltpu.make_async_copy(h_hbm, hbuf, h_sem.at[0])
     pat_load = pltpu.make_async_copy(pattern_hbm, patterns.at[role], pat_own.at[0])
 
     barrier = pltpu.get_barrier_semaphore()
-    for e in range(GROUP - 1):
+    for e in range(1, GROUP - 1):
         pl.semaphore_signal(barrier, inc=1, device_id=to_peer(peers[e]), device_id_type=MESH)
     pl.semaphore_signal(barrier, inc=1, device_id={"section": partner}, device_id_type=MESH)
 
@@ -232,22 +258,36 @@
         q_local(n).start()
 
     pl.semaphore_wait(
-        barrier, GROUP + has_prev.astype(jnp.int32) + has_next.astype(jnp.int32)
+        barrier, GROUP - 1 + has_prev.astype(jnp.int32) + has_next.astype(jnp.int32)
     )
 
-    for e in range(GROUP - 1):
+    pl.semaphore_signal(entered, inc=1, device_id=to_peer(peers[1]), device_id_type=MESH)
+
+    def send(kind, n, e):
+        if kind == 2:
+            q_copy(n, e).start()
+        else:
+            kv_copy(kind, n, e).start()
+
+    for e in (1, 2):
         pat_copy(e).start()
+        send(0, 0, e)
+    z_start(0, 0, role, True)
+    z_start(1, 0, role, True)
+    pl.semaphore_wait(entered, 1)
+    pat_copy(0).start()
+    send(0, 0, 0)
     for n in range(heads):
-        for i in range(2):
-            for e in range(GROUP - 1):
-                kv_copy(i, n, e).start()
-            if n < 2:
-                z_start(i, n, role, True)
-        for e in range(GROUP - 1):
-            q_copy(n, e).start()
+        for kind in range(3):
+            if n + kind > 0:
+                for e in range(GROUP - 1):
+                    send(kind, n, e)
+                if n == 1 and kind < 2:
+                    z_start(kind, n, role, True)
     for n in range(heads):
         for c in range(GROUP):
             w_copy(n, c).start()
+            w_local(n, c).start()
     h_load.start()
 
     @pl.when(jnp.logical_not(has_prev))
@@ -278,33 +318,29 @@
                 bias[c, i * BLOCK : (i + 1) * BLOCK, g * BLOCK : (g + 1) * BLOCK] = value
 
     factor = math.log2(math.e) / math.sqrt(HEAD_DIM)
-    tile = math.gcd(model, 1024)
+    tile = math.gcd(features, 512)
 
     def forward(n):
         for i in range(2):
-            kv_local(i, n).wait()
-        for e in (1, 2, 0):
-            for i in range(2):
+            for e in (1, 2, 0):
                 kv_arrive(i, n, GROUP + peers[e])
                 z_start(i, n, peers[e], False)
+        for i in range(2):
+            kv_local(i, n).wait()
 
         @pl.when(n + 2 < heads)
         def _():
             for i in range(2):
                 z_start(i, jnp.minimum(n + 2, heads - 1), role, True)
 
-    def unit(n, c):
-        @pl.when(c == role)
-        def _():
+    def unit(n, e):
+        c = role if e is None else peers[e]
+        if e is None:
             q_local(n).wait()
-
-        @pl.when(c != role)
-        def _():
+        else:
             q_arrive(n, c)
-
-        z_arrive(n, c)
-        keys_at = pl.ds(c * rows + skip, span)
-        query = qbuf[n, c * rows : (c + 1) * rows, :]
+        keys_at = pl.ds(pl.multiple_of(c * rows + skip, BLOCK), span)
+        query = qbuf[n, place(c), :]
         scores = lax.dot_general(
             query, kv[0, n, keys_at, :], (((1,), (1,)), ((), ())),
             preferred_element_type=jnp.float32,
@@ -319,102 +355,91 @@
         )
         result = (mixture / total).astype(jnp.bfloat16)
 
-        @pl.when(c == role)
-        def _():
-            amix[n, :, mix_cols(c)] = result
-
-        @pl.when(c != role)
-        def _():
-            obuf[n, c * rows : (c + 1) * rows, :] = result
+        if e is None:
+            amix[0, n, :, mix_cols(c)] = result
+        else:
+            obuf[n, place(c), :] = result
             o_copy(n, c).start()
 
-    def mixed_ready(n):
+    def project_own(n, first):
         for e in range(GROUP - 1):
             o_arrive(n, peers[e])
-
-    def depth(n):
-        return pl.ds(pl.multiple_of(n * GROUP * HEAD_DIM, GROUP * HEAD_DIM), GROUP * HEAD_DIM)
-
-    def project(n, first):
+        mix_copy(n, 0, GROUP).start()
         for c in range(GROUP):
-            w_copy(n, c).wait()
-        mixed_ready(n)
-        for t in range(0, model, tile):
+            w_local(n, c).wait()
+        for t in range(0, features, tile):
             value = jnp.dot(
-                amix[n], wbuf[depth(n), t : t + tile], preferred_element_type=jnp.float32
+                amix[0, n], wbuf[0, n, :, t : t + tile], preferred_element_type=jnp.float32
             )
             if first:
                 acc[:, t : t + tile] = value
             else:
                 acc[:, t : t + tile] += value
 
+    def project_other(n):
+        for c in range(GROUP):
+            w_copy(n, c).wait_recv()
+        mix_copy(n, 0, GROUP).wait_recv()
+        for t in range(0, features, tile):
+            acc[:, t : t + tile] += jnp.dot(
+                amix[1, n], wbuf[1, n, :, t : t + tile], preferred_element_type=jnp.float32
+            )
+
+    last = heads - 1
+
+    def chunk(n):
+        for c in reversed(range(GROUP)):
+            z_arrive(n, c)
+        for e in range(GROUP - 1):
+            unit(n, e)
+
     @pl.loop(0, heads)
-    def _(t):
-        forward(t)
-
-        @pl.when(t >= 1)
+    def _(n):
+        forward(n)
+
+        @pl.when(n >= 1)
         def _():
-            for c in reversed(range(GROUP)):
-                unit(t - 1, c)
-
-    last_head = heads - 1
-    for c in reversed(range(GROUP)):
-        unit(last_head, c)
-    for n in range(last_head):
-        project(n, n == 0)
+            chunk(n - 1)
+            unit(n - 1, None)
+
+    project_own(0, True)
+    chunk(last)
+    if last > 1:
+        project_own(1, False)
+    project_other(0)
+    unit(last, None)
+    for n in range(1, last):
+        if n > 1:
+            project_own(n, False)
+        project_other(n)
     h_load.wait()
+
     for c in range(GROUP):
-        w_copy(last_head, c).wait()
-    mixed_ready(last_head)
-
-    pieces = part_send.shape[0]
-    part_cols = width // pieces
-
-    def part_copy(c):
-        cols = pl.ds(c * part_cols, part_cols)
-        return pltpu.make_async_remote_copy(
-            src_ref=outgoing.at[:, cols],
-            dst_ref=incoming.at[:, cols],
-            send_sem=part_send.at[c],
-            recv_sem=part_recv.at[c],
-            device_id={"section": partner},
-            device_id_type=MESH,
-        )
-
-    def last_sum(start):
-        cols = pl.ds(pl.multiple_of(start, part_cols), part_cols)
-        return acc[:, cols] + jnp.dot(
-            amix[last_head], wbuf[depth(last_head), cols], preferred_element_type=jnp.float32
-        )
-
-    for c in range(pieces):
-        outgoing[:, c * part_cols : (c + 1) * part_cols] = last_sum(
-            partner * width + c * part_cols
-        ).astype(outgoing.dtype)
-        if c >= 1:
-            part_copy(c - 1).start()
-    for c in range(pieces):
-        cols = slice(c * part_cols, (c + 1) * part_cols)
-        mine[:, cols] = last_sum(section * width + c * part_cols).astype(mine.dtype)
-        if c == 0:
-            part_copy(pieces - 1).start()
-    for c in range(pieces):
-        part_copy(c).wait_recv()
-
-    strip = 16
-
-    @pl.loop(0, rows // strip)
-    def _(i):
-        at = pl.ds(pl.multiple_of(i * strip, strip), strip)
-        here = mine[at, :].astype(jnp.float32)
-        there = incoming[at, :].astype(jnp.float32)
-        stream = hbuf[at, :].astype(jnp.float32) + (here + there)
-        stream_ref[at, :] = stream
+        w_local(last, c).wait()
+        w_copy(last, c).wait_recv()
+
+        @pl.when(c != role)
+        def _():
+            o_arrive(last, c)
+
+        mix_copy(last, c, 1).start()
+    for t in range(0, features, tile):
+        acc[:, t : t + tile] += jnp.dot(
+            amix[0, last], wbuf[0, last, :, t : t + tile], preferred_element_type=jnp.float32
+        )
+    for c in range(GROUP):
+        mix_copy(last, c, 1).wait_recv()
+    lanes = jnp.zeros(square_out.shape, jnp.float32)
+    for t in range(0, features, tile):
+        value = acc[:, t : t + tile] + jnp.dot(
+            amix[1, last], wbuf[1, last, :, t : t + tile], preferred_element_type=jnp.float32
+        )
+        stream = hbuf[:, t : t + tile].astype(jnp.float32) + value
+        stream_ref[:, t : t + tile] = stream
         squares = stream * stream
-        lanes = squares[:, 0:128]
-        for c in range(128, width, 128):
-            lanes = lanes + squares[:, c : c + 128]
-        square_out[at, :] = lanes
+        for p in range(0, tile, 128):
+            lanes = lanes + squares[:, p : p + 128]
+    square_out[...] = lanes
 
     square_copy = pltpu.make_async_remote_copy(
         src_ref=square_out,
@@ -440,8 +465,13 @@
             for c in range(GROUP):
                 z_end(i, n, c)
 
-    for c in range(pieces):
-        part_copy(c).wait_send()
+    for n in range(heads):
+        for c in range(GROUP):
+            w_copy(n, c).wait_send()
+            if n == last:
+                mix_copy(n, c, 1).wait_send()
+        if n < last:
+            mix_copy(n, 0, GROUP).wait_send()
     square_copy.wait()
     square_ref[...] = square_out[...] + square_in[...]
 
@@ -450,7 +480,7 @@
     rows, width = queries.shape
     model = out_weight.shape[1]
     heads = width // (GROUP * HEAD_DIM)
-    pieces = 4
+    features = hidden.shape[1]
     span = (WINDOW_BLOCKS - 1) * BLOCK + rows
     anywhere = pl.BlockSpec(memory_space=pl.ANY)
     vmem = pl.BlockSpec(memory_space=pltpu.VMEM)
@@ -458,7 +488,7 @@
     stream, squares = pl.pallas_call(
         kernel,
         out_shape=(
-            jax.ShapeDtypeStruct((rows, width), jnp.float32),
+            jax.ShapeDtypeStruct((rows, features), jnp.float32),
             jax.ShapeDtypeStruct((rows, 128), jnp.float32),
         ),
         in_specs=[anywhere] * 6,
@@ -467,21 +497,20 @@
             pltpu.VMEM((2, heads, 2 * GROUP * rows, HEAD_DIM), bf16),
             pltpu.VMEM((heads, GROUP * rows, HEAD_DIM), bf16),
             pltpu.VMEM((heads, GROUP * rows, HEAD_DIM), bf16),
-            pltpu.VMEM((heads, rows, GROUP * HEAD_DIM), bf16),
-            pltpu.VMEM((width, model), bf16),
-            pltpu.VMEM((rows, width), bf16),
+            pltpu.VMEM((2, heads, rows, GROUP * HEAD_DIM), bf16),
+            pltpu.VMEM((2, heads, GROUP * HEAD_DIM, features), bf16),
+            pltpu.VMEM((rows, features), bf16),
             pltpu.VMEM((GROUP,) + block_pattern.shape, jnp.int32),
             pltpu.VMEM((GROUP, rows, span), jnp.float32),
-            pltpu.VMEM((rows, model), jnp.float32),
-            pltpu.VMEM((rows, width), bf16),
-            pltpu.VMEM((rows, width), bf16),
-            pltpu.VMEM((rows, width), bf16),
+            pltpu.VMEM((rows, features), jnp.float32),
             pltpu.VMEM((rows, 128), jnp.float32),
             pltpu.VMEM((rows, 128), jnp.float32),
             pltpu.SemaphoreType.DMA((2, heads)),
             pltpu.SemaphoreType.DMA((heads,)),
             pltpu.SemaphoreType.DMA((1,)),
             pltpu.SemaphoreType.DMA((heads, GROUP)),
+            pltpu.SemaphoreType.DMA((heads, GROUP)),
+            pltpu.SemaphoreType.DMA((heads, GROUP)),
             pltpu.SemaphoreType.DMA((1,)),
             pltpu.SemaphoreType.DMA((2, heads, GROUP - 1)),
             pltpu.SemaphoreType.DMA((2, heads, 2 * GROUP)),
@@ -492,14 +521,22 @@
             pltpu.SemaphoreType.DMA((heads, GROUP)),
             pltpu.SemaphoreType.DMA((GROUP - 1,)),
             pltpu.SemaphoreType.DMA((GROUP,)),
-            pltpu.SemaphoreType.DMA((pieces,)),
-            pltpu.SemaphoreType.DMA((pieces,)),
+            pltpu.SemaphoreType.DMA((heads, GROUP)),
+            pltpu.SemaphoreType.DMA((heads, GROUP)),
             pltpu.SemaphoreType.DMA((2,)),
+            pltpu.SemaphoreType.REGULAR,
         ],
         compiler_params=pltpu.CompilerParams(
-            collective_id=0, has_side_effects=True, vmem_limit_bytes=62 * 1024 * 1024
+            collective_id=0, has_side_effects=True, vmem_limit_bytes=40 * 1024 * 1024
         ),
-    )(queries, key_rows, value_rows, block_pattern, out_weight, hidden)
+    )(
+        *[
+            pltpu.with_memory_space_constraint(value, pltpu.HBM)
+            for value in (
+                queries, key_rows, value_rows, block_pattern, out_weight, hidden
+            )
+        ]
+    )
     mean_square = jnp.sum(squares, axis=1, keepdims=True) / model
     normed = stream * lax.rsqrt(mean_square + 1e-06) * norm_gain[None, :]
     return (stream.astype(jnp.bfloat16), normed.astype(jnp.bfloat16))

time: 66.9 us -> 60.2 us (0.90)
  Pallas kernels: 61.2 us -> 57.6 us
  other arithmetic: 4.8 us -> 1.77 us
    pallas_call x1, Pallas kernels: 61.2 us -> 57.6 us  [shards(): pl.pallas_call(kernel, out_shape=(jax.ShapeDtypeStruct((rows, features),...]
    convert_element_type x1, other arithmetic: 3.78 us -> 1.66 us  [shards(): return (stream.astype(jnp.bfloat16), normed.astype(jnp.bfloat16))]
    reduce_sum x1, other arithmetic: 1.02 us -> 0.11 us  [shards(): mean_square = jnp.sum(squares, axis=1, keepdims=True) / model]
where the time goes in v2:
time: 60.2 us; the launch traced here: 60 us
  Pallas kernels  57.6 us (96%)
  other arithmetic  1.77 us (3%)
  between operations  0.67 us (1%)
    pallas_call x1, Pallas kernels, shards(): pl.pallas_call(kernel, out_shape=(jax.ShapeDtypeStruct((rows, features),...  57.6 us
    convert_element_type x1, other arithmetic, shards(): return (stream.astype(jnp.bfloat16), normed.astype(jnp.bfloat16))  1.66 us

profile of v2, /device:TPU:25, one launch (start us, length us, event | category | flops | bytes accessed | tf_op | source)
XLA Modules:
  0.0 60.0 jit_solution(2144398487673604629)
XLA Ops:
  0.6 0.0 copy-start
  0.6 57.6 %shard_map.86 = (f32[256,2048]{1,0:T(8,128)S(1)}, f32[256,128]{1,0:T(8,128)S(1)}) custom-call(bf16[256,2048]{1,0:T(8,128)(2,1)} %q_hbm.1, bf16[256,2048]{1,0:T(8,128)(2,1)} %k_hbm.1, bf16[256,2048]{1,0:T(8,128)(2,1)} %v_hbm.1, s32[2,8]{1,0:T(2,128)} %pattern_hbm.1, bf16[2048,4096]{1,0:T(8,128)(2,1)} %w_hbm.1, bf16[256,2048]{1,0:T(8,128)(2,1)} %h_hbm.1), custom_call_target="tpu_custom_call" | custom-call | tf_op jit(solution)/shard_map/pallas_call | solution.py:488
  58.2 0.1 reduce_sum.9
  58.4 0.0 copy-done
  58.4 1.7 %multiply_convert_fusion = (bf16[256,2048]{1,0:T(8,128)(2,1)}, bf16[256,2048]{1,0:T(8,128)(2,1)}) fusion(f32[256,2048]{1,0:T(8,128)S(1)} %get-tuple-element.4, f32[2048]{0:T(1024)S(1)} %copy-done, f32[256]{0:T(256)S(1)} %add_rsqrt_fusion), kind=kLoop, calls=%fused_computation | loop fusion | flops 2097152 | bytes 4203520 | tf_op jit(solution)/shard_map/convert_element_type | solution.py:542
  (1 shorter events, 0.0 us)
Async XLA Ops:
  0.6 57.7 %copy-start = (f32[2048]{0:T(1024)S(1)}, f32[2048]{0:T(1024)}, u32[]{:S(2)}) copy-start(f32[2048]{0:T(1024)} %param.13) | copy-start | bytes 24580

commit v3 on v2

--- a/solution.py
+++ b/solution.py
@@ -221,7 +221,7 @@
         )
 
     def mix_copy(n, first, extent):
-        cols = pl.ds(first * HEAD_DIM, extent * HEAD_DIM)
+        cols = pl.ds(pl.multiple_of(first * HEAD_DIM, HEAD_DIM), extent * HEAD_DIM)
         return pltpu.make_async_remote_copy(
             src_ref=amix.at[0, n, :, cols],
             dst_ref=amix.at[1, n, :, cols],
@@ -333,16 +333,10 @@
             for i in range(2):
                 z_start(i, jnp.minimum(n + 2, heads - 1), role, True)
 
-    def unit(n, e):
-        c = role if e is None else peers[e]
-        if e is None:
-            q_local(n).wait()
-        else:
-            q_arrive(n, c)
+    def attend(n, c):
         keys_at = pl.ds(pl.multiple_of(c * rows + skip, BLOCK), span)
-        query = qbuf[n, place(c), :]
         scores = lax.dot_general(
-            query, kv[0, n, keys_at, :], (((1,), (1,)), ((), ())),
+            qbuf[n, place(c), :], kv[0, n, keys_at, :], (((1,), (1,)), ((), ())),
             preferred_element_type=jnp.float32,
         )
         scores = scores + bias[c]
@@ -353,13 +347,23 @@
             exponent.astype(jnp.bfloat16), kv[1, n, keys_at, :],
             preferred_element_type=jnp.float32,
         )
-        result = (mixture / total).astype(jnp.bfloat16)
-
-        if e is None:
-            amix[0, n, :, mix_cols(c)] = result
-        else:
-            obuf[n, place(c), :] = result
-            o_copy(n, c).start()
+        return (mixture / total).astype(jnp.bfloat16)
+
+    def units(n, chosen):
+        for e in chosen:
+            if e is None:
+                q_local(n).wait()
+            else:
+                q_arrive(n, peers[e])
+        results = [attend(n, role if e is None else peers[e]) for e in chosen]
+        for e, result in zip(chosen, results):
+            if e is None:
+                amix[0, n, :, mix_cols(role)] = result
+            else:
+                obuf[n, place(peers[e]), :] = result
+        for e in chosen:
+            if e is not None:
+                o_copy(n, peers[e]).start()
 
     def project_own(n, first):
         for e in range(GROUP - 1):
@@ -390,8 +394,8 @@
     def chunk(n):
         for c in reversed(range(GROUP)):
             z_arrive(n, c)
-        for e in range(GROUP - 1):
-            unit(n, e)
+        for e in (0, 1, 2, None):
+            units(n, (e,))
 
     @pl.loop(0, heads)
     def _(n):
@@ -400,29 +404,24 @@
         @pl.when(n >= 1)
         def _():
             chunk(n - 1)
-            unit(n - 1, None)
 
     project_own(0, True)
     chunk(last)
-    if last > 1:
-        project_own(1, False)
+    mix_copy(last, role, 1).start()
     project_other(0)
-    unit(last, None)
     for n in range(1, last):
+        project_own(n, False)
         if n > 1:
-            project_own(n, False)
-        project_other(n)
+            project_other(n - 1)
     h_load.wait()
-
     for c in range(GROUP):
         w_local(last, c).wait()
         w_copy(last, c).wait_recv()
-
-        @pl.when(c != role)
-        def _():
-            o_arrive(last, c)
-
-        mix_copy(last, c, 1).start()
+    for e in range(GROUP - 1):
+        o_arrive(last, peers[e])
+        mix_copy(last, peers[e], 1).start()
+    if last > 1:
+        project_other(last - 1)
     for t in range(0, features, tile):
         acc[:, t : t + tile] += jnp.dot(
             amix[0, last], wbuf[0, last, :, t : t + tile], preferred_element_type=jnp.float32

time: 60.2 us -> 58.8 us (0.977)
  Pallas kernels: 57.6 us -> 56.2 us
    pallas_call x1, Pallas kernels: 57.6 us -> 56.2 us  [shards(): pl.pallas_call(kernel, out_shape=(jax.ShapeDtypeStruct((rows, features),...]
where the time goes in v3:
time: 58.8 us; the launch traced here: 58.6 us
  Pallas kernels  56.2 us (96%)
  other arithmetic  1.77 us (3%)
  between operations  0.67 us (1%)
    pallas_call x1, Pallas kernels, shards(): pl.pallas_call(kernel, out_shape=(jax.ShapeDtypeStruct((rows, features),...  56.2 us
    convert_element_type x1, other arithmetic, shards(): return (stream.astype(jnp.bfloat16), normed.astype(jnp.bfloat16))  1.66 us

profile of v3, /device:TPU:25, one launch (start us, length us, event | category | flops | bytes accessed | tf_op | source)
XLA Modules:
  0.0 58.6 jit_solution(14655105668881180445)
XLA Ops:
  0.6 0.0 copy-start
  0.6 56.2 %shard_map.86 = (f32[256,2048]{1,0:T(8,128)S(1)}, f32[256,128]{1,0:T(8,128)S(1)}) custom-call(bf16[256,2048]{1,0:T(8,128)(2,1)} %q_hbm.1, bf16[256,2048]{1,0:T(8,128)(2,1)} %k_hbm.1, bf16[256,2048]{1,0:T(8,128)(2,1)} %v_hbm.1, s32[2,8]{1,0:T(2,128)} %pattern_hbm.1, bf16[2048,4096]{1,0:T(8,128)(2,1)} %w_hbm.1, bf16[256,2048]{1,0:T(8,128)(2,1)} %h_hbm.1), custom_call_target="tpu_custom_call" | custom-call | tf_op jit(solution)/shard_map/pallas_call | solution.py:487
  56.8 0.1 reduce_sum.9
  57.0 0.0 copy-done
  57.0 1.7 %multiply_convert_fusion = (bf16[256,2048]{1,0:T(8,128)(2,1)}, bf16[256,2048]{1,0:T(8,128)(2,1)}) fusion(f32[256,2048]{1,0:T(8,128)S(1)} %get-tuple-element.4, f32[2048]{0:T(1024)S(1)} %copy-done, f32[256]{0:T(256)S(1)} %add_rsqrt_fusion), kind=kLoop, calls=%fused_computation | loop fusion | flops 2097152 | bytes 4203520 | tf_op jit(solution)/shard_map/convert_element_type | solution.py:541
  (1 shorter events, 0.0 us)
Async XLA Ops:
  0.6 56.3 %copy-start = (f32[2048]{0:T(1024)S(1)}, f32[2048]{0:T(1024)}, u32[]{:S(2)}) copy-start(f32[2048]{0:T(1024)} %param.13) | copy-start | bytes 24580

commit v4 on v3

--- a/solution.py
+++ b/solution.py
@@ -104,13 +104,14 @@
             device_id_type=MESH,
         ).wait_recv()
 
-    def mix_cols(c):
-        return pl.ds(pl.multiple_of(c * HEAD_DIM, HEAD_DIM), HEAD_DIM)
+    def mixed(k, n, c, extent=1):
+        start = ((2 * n + k) * GROUP + c) * HEAD_DIM
+        return pl.ds(pl.multiple_of(start, HEAD_DIM), extent * HEAD_DIM)
 
     def o_copy(n, c):
         return pltpu.make_async_remote_copy(
             src_ref=obuf.at[n, place(c), :],
-            dst_ref=amix.at[0, n, :, mix_cols(role)],
+            dst_ref=amix.at[:, mixed(0, n, role)],
             send_sem=o_send.at[n, c],
             recv_sem=o_recv.at[n, role],
             device_id=to_peer(c),
@@ -119,8 +120,8 @@
 
     def o_arrive(n, c):
         pltpu.make_async_remote_copy(
-            src_ref=amix.at[0, n, :, mix_cols(c)],
-            dst_ref=amix.at[0, n, :, mix_cols(c)],
+            src_ref=amix.at[:, mixed(0, n, c)],
+            dst_ref=amix.at[:, mixed(0, n, c)],
             send_sem=o_send.at[n, 0],
             recv_sem=o_recv.at[n, c],
             device_id={"section": partner},
@@ -206,14 +207,14 @@
     def w_local(n, c):
         return pltpu.make_async_copy(
             w_part(n, c, section),
-            wbuf.at[0, n, c * HEAD_DIM : (c + 1) * HEAD_DIM, :],
+            wbuf.at[mixed(0, n, c), :],
             w_own.at[n, c],
         )
 
     def w_copy(n, c):
         return pltpu.make_async_remote_copy(
             src_ref=w_part(n, c, partner),
-            dst_ref=wbuf.at[1, n, c * HEAD_DIM : (c + 1) * HEAD_DIM, :],
+            dst_ref=wbuf.at[mixed(1, n, c), :],
             send_sem=w_send.at[n, c],
             recv_sem=w_recv.at[n, c],
             device_id={"section": partner},
@@ -221,10 +222,9 @@
         )
 
     def mix_copy(n, first, extent):
-        cols = pl.ds(pl.multiple_of(first * HEAD_DIM, HEAD_DIM), extent * HEAD_DIM)
         return pltpu.make_async_remote_copy(
-            src_ref=amix.at[0, n, :, cols],
-            dst_ref=amix.at[1, n, :, cols],
+            src_ref=amix.at[:, mixed(0, n, first, extent)],
+            dst_ref=amix.at[:, mixed(1, n, first, extent)],
             send_sem=mix_send.at[n, first],
             recv_sem=mix_recv.at[n, first],
             device_id={"section": partner},
@@ -284,6 +284,13 @@
                     send(kind, n, e)
                 if n == 1 and kind < 2:
                     z_start(kind, n, role, True)
+        if n == 0:
+            @pl.when(role == 0)
+            def _():
+                for m in range(2, heads):
+                    for i in range(2):
+                        z_start(i, m, role, True)
+
     for n in range(heads):
         for c in range(GROUP):
             w_copy(n, c).start()
@@ -328,7 +335,7 @@
         for i in range(2):
             kv_local(i, n).wait()
 
-        @pl.when(n + 2 < heads)
+        @pl.when((n + 2 < heads) & (role > 0))
         def _():
             for i in range(2):
                 z_start(i, jnp.minimum(n + 2, heads - 1), role, True)
@@ -339,15 +346,15 @@
             qbuf[n, place(c), :], kv[0, n, keys_at, :], (((1,), (1,)), ((), ())),
             preferred_element_type=jnp.float32,
         )
-        scores = scores + bias[c]
+        scores = scores * factor + bias[c]
         largest = jnp.max(scores, axis=1, keepdims=True)
-        exponent = jnp.exp2((scores - largest) * factor)
+        exponent = jnp.exp2(scores - largest)
         total = jnp.sum(exponent, axis=1, keepdims=True)
         mixture = jnp.dot(
             exponent.astype(jnp.bfloat16), kv[1, n, keys_at, :],
             preferred_element_type=jnp.float32,
         )
-        return (mixture / total).astype(jnp.bfloat16)
+        return (mixture * (1.0 / total)).astype(jnp.bfloat16)
 
     def units(n, chosen):
         for e in chosen:
@@ -358,38 +365,43 @@
         results = [attend(n, role if e is None else peers[e]) for e in chosen]
         for e, result in zip(chosen, results):
             if e is None:
-                amix[0, n, :, mix_cols(role)] = result
+                amix[:, mixed(0, n, role)] = result
             else:
                 obuf[n, place(peers[e]), :] = result
         for e in chosen:
             if e is not None:
                 o_copy(n, peers[e]).start()
 
-    def project_own(n, first):
+    chunk_depth = GROUP * HEAD_DIM
+    last = heads - 1
+    hold = max(last - 1, 1)
+
+    def product(block, extent, t):
+        depth = slice(block * chunk_depth, (block + extent) * chunk_depth)
+        return jnp.dot(
+            amix[:, depth], wbuf[depth, t : t + tile], preferred_element_type=jnp.float32
+        )
+
+    def project(block, extent, first=False):
+        for t in range(0, features, tile):
+            if first:
+                acc[:, t : t + tile] = hbuf[:, t : t + tile].astype(jnp.float32) + product(
+                    block, extent, t
+                )
+            else:
+                acc[:, t : t + tile] += product(block, extent, t)
+
+    def own_ready(n):
         for e in range(GROUP - 1):
             o_arrive(n, peers[e])
         mix_copy(n, 0, GROUP).start()
         for c in range(GROUP):
             w_local(n, c).wait()
-        for t in range(0, features, tile):
-            value = jnp.dot(
-                amix[0, n], wbuf[0, n, :, t : t + tile], preferred_element_type=jnp.float32
-            )
-            if first:
-                acc[:, t : t + tile] = value
-            else:
-                acc[:, t : t + tile] += value
-
-    def project_other(n):
+
+    def other_ready(n):
         for c in range(GROUP):
             w_copy(n, c).wait_recv()
         mix_copy(n, 0, GROUP).wait_recv()
-        for t in range(0, features, tile):
-            acc[:, t : t + tile] += jnp.dot(
-                amix[1, n], wbuf[1, n, :, t : t + tile], preferred_element_type=jnp.float32
-            )
-
-    last = heads - 1
 
     def chunk(n):
         for c in reversed(range(GROUP)):
@@ -405,35 +417,30 @@
         def _():
             chunk(n - 1)
 
-    project_own(0, True)
-    chunk(last)
-    mix_copy(last, role, 1).start()
-    project_other(0)
-    for n in range(1, last):
-        project_own(n, False)
-        if n > 1:
-            project_other(n - 1)
-    h_load.wait()
+    for n in range(last):
+        if n == max(last - 2, 0):
+            chunk(last)
+            mix_copy(last, role, 1).start()
+        own_ready(n)
+        if n == 0:
+            h_load.wait()
+            project(0, 1, True)
+        else:
+            other_ready(n - 1)
+            project(2 * n - 1, 2)
     for c in range(GROUP):
         w_local(last, c).wait()
         w_copy(last, c).wait_recv()
     for e in range(GROUP - 1):
         o_arrive(last, peers[e])
         mix_copy(last, peers[e], 1).start()
-    if last > 1:
-        project_other(last - 1)
-    for t in range(0, features, tile):
-        acc[:, t : t + tile] += jnp.dot(
-            amix[0, last], wbuf[0, last, :, t : t + tile], preferred_element_type=jnp.float32
-        )
+    other_ready(last - 1)
+    project(2 * last - 1, 2)
     for c in range(GROUP):
         mix_copy(last, c, 1).wait_recv()
     lanes = jnp.zeros(square_out.shape, jnp.float32)
     for t in range(0, features, tile):
-        value = acc[:, t : t + tile] + jnp.dot(
-            amix[1, last], wbuf[1, last, :, t : t + tile], preferred_element_type=jnp.float32
-        )
-        stream = hbuf[:, t : t + tile].astype(jnp.float32) + value
+        stream = acc[:, t : t + tile] + product(2 * last + 1, 1, t)
         stream_ref[:, t : t + tile] = stream
         squares = stream * stream
         for p in range(0, tile, 128):
@@ -496,8 +503,8 @@
             pltpu.VMEM((2, heads, 2 * GROUP * rows, HEAD_DIM), bf16),
             pltpu.VMEM((heads, GROUP * rows, HEAD_DIM), bf16),
             pltpu.VMEM((heads, GROUP * rows, HEAD_DIM), bf16),
-            pltpu.VMEM((2, heads, rows, GROUP * HEAD_DIM), bf16),
-            pltpu.VMEM((2, heads, GROUP * HEAD_DIM, features), bf16),
+            pltpu.VMEM((rows, 2 * width), bf16),
+            pltpu.VMEM((2 * width, features), bf16),
             pltpu.VMEM((rows, features), bf16),
             pltpu.VMEM((GROUP,) + block_pattern.shape, jnp.int32),
             pltpu.VMEM((GROUP, rows, span), jnp.float32),

time: 58.8 us -> 58.8 us (level); the launches traced: 58.6 us -> 57.9 us
  Pallas kernels: 56.2 us -> 55.5 us
    pallas_call x1, Pallas kernels: 56.2 us -> 55.5 us  [shards(): pl.pallas_call(kernel, out_shape=(jax.ShapeDtypeStruct((rows, features),...]
where the time goes in v4:
time: 58.8 us; the launch traced here: 57.9 us
  Pallas kernels  55.5 us (94%)
  other arithmetic  1.77 us (3%)
  between operations  0.67 us (1%)
    pallas_call x1, Pallas kernels, shards(): pl.pallas_call(kernel, out_shape=(jax.ShapeDtypeStruct((rows, features),...  55.5 us
    convert_element_type x1, other arithmetic, shards(): return (stream.astype(jnp.bfloat16), normed.astype(jnp.bfloat16))  1.66 us

profile of v4, /device:TPU:25, one launch (start us, length us, event | category | flops | bytes accessed | tf_op | source)
XLA Modules:
  0.0 57.9 jit_solution(10383896570865556011)
XLA Ops:
  0.6 0.0 copy-start
  0.6 55.5 %shard_map.86 = (f32[256,2048]{1,0:T(8,128)S(1)}, f32[256,128]{1,0:T(8,128)S(1)}) custom-call(bf16[256,2048]{1,0:T(8,128)(2,1)} %q_hbm.1, bf16[256,2048]{1,0:T(8,128)(2,1)} %k_hbm.1, bf16[256,2048]{1,0:T(8,128)(2,1)} %v_hbm.1, s32[2,8]{1,0:T(2,128)} %pattern_hbm.1, bf16[2048,4096]{1,0:T(8,128)(2,1)} %w_hbm.1, bf16[256,2048]{1,0:T(8,128)(2,1)} %h_hbm.1), custom_call_target="tpu_custom_call" | custom-call | tf_op jit(solution)/shard_map/pallas_call | solution.py:494
  56.2 0.1 reduce_sum.9
  56.3 0.0 copy-done
  56.3 1.7 %multiply_convert_fusion = (bf16[256,2048]{1,0:T(8,128)(2,1)}, bf16[256,2048]{1,0:T(8,128)(2,1)}) fusion(f32[256,2048]{1,0:T(8,128)S(1)} %get-tuple-element.4, f32[2048]{0:T(1024)S(1)} %copy-done, f32[256]{0:T(256)S(1)} %add_rsqrt_fusion), kind=kLoop, calls=%fused_computation | loop fusion | flops 2097152 | bytes 4203520 | tf_op jit(solution)/shard_map/convert_element_type | solution.py:548
  (1 shorter events, 0.0 us)
Async XLA Ops:
  0.6 55.6 %copy-start = (f32[2048]{0:T(1024)S(1)}, f32[2048]{0:T(1024)}, u32[]{:S(2)}) copy-start(f32[2048]{0:T(1024)} %param.13) | copy-start | bytes 24580

commit v5 on v4

--- a/solution.py
+++ b/solution.py
@@ -270,13 +270,13 @@
             kv_copy(kind, n, e).start()
 
     for e in (1, 2):
+        send(0, 0, e)
         pat_copy(e).start()
-        send(0, 0, e)
     z_start(0, 0, role, True)
     z_start(1, 0, role, True)
     pl.semaphore_wait(entered, 1)
+    send(0, 0, 0)
     pat_copy(0).start()
-    send(0, 0, 0)
     for n in range(heads):
         for kind in range(3):
             if n + kind > 0:

time: 58.8 us -> 58.7 us (level)
  no operation moved by 1% of the time
where the time goes in v5:
time: 58.7 us; the launch traced here: 57.8 us
  Pallas kernels  55.3 us (94%)
  other arithmetic  1.77 us (3%)
  between operations  0.67 us (1%)
    pallas_call x1, Pallas kernels, shards(): pl.pallas_call(kernel, out_shape=(jax.ShapeDtypeStruct((rows, features),...  55.3 us
    convert_element_type x1, other arithmetic, shards(): return (stream.astype(jnp.bfloat16), normed.astype(jnp.bfloat16))  1.66 us

profile of v5, /device:TPU:25, one launch (start us, length us, event | category | flops | bytes accessed | tf_op | source)
XLA Modules:
  0.0 57.8 jit_solution(8272935998428886714)
XLA Ops:
  0.6 0.0 copy-start
  0.6 55.3 %shard_map.86 = (f32[256,2048]{1,0:T(8,128)S(1)}, f32[256,128]{1,0:T(8,128)S(1)}) custom-call(bf16[256,2048]{1,0:T(8,128)(2,1)} %q_hbm.1, bf16[256,2048]{1,0:T(8,128)(2,1)} %k_hbm.1, bf16[256,2048]{1,0:T(8,128)(2,1)} %v_hbm.1, s32[2,8]{1,0:T(2,128)} %pattern_hbm.1, bf16[2048,4096]{1,0:T(8,128)(2,1)} %w_hbm.1, bf16[256,2048]{1,0:T(8,128)(2,1)} %h_hbm.1), custom_call_target="tpu_custom_call" | custom-call | tf_op jit(solution)/shard_map/pallas_call | solution.py:494
  56.0 0.1 reduce_sum.9
  56.1 0.0 copy-done
  56.1 1.7 %multiply_convert_fusion = (bf16[256,2048]{1,0:T(8,128)(2,1)}, bf16[256,2048]{1,0:T(8,128)(2,1)}) fusion(f32[256,2048]{1,0:T(8,128)S(1)} %get-tuple-element.4, f32[2048]{0:T(1024)S(1)} %copy-done, f32[256]{0:T(256)S(1)} %add_rsqrt_fusion), kind=kLoop, calls=%fused_computation | loop fusion | flops 2097152 | bytes 4203520 | tf_op jit(solution)/shard_map/convert_element_type | solution.py:548
  (1 shorter events, 0.0 us)
Async XLA Ops:
  0.6 55.5 %copy-start = (f32[2048]{0:T(1024)S(1)}, f32[2048]{0:T(1024)}, u32[]{:S(2)}) copy-start(f32[2048]{0:T(1024)} %param.13) | copy-start | bytes 24580
